TPU v7x, 32 devices: a whole 2x2x4 slice. The times are simulated.
32 devices in a mesh: expert: 8 (over z, x), fsdp: 4 (over y, core).
Axes of the slice: x: 2, y: 2, z: 4, core: 2. Of those that a mesh axis runs over, the one named last changes fastest.
Arguments:
- tokens: bfloat16 [2048, 7168], P('expert', 'fsdp'), may hold values from -6 to 6
- output_grad: bfloat16 [2048, 7168], P('expert', 'fsdp'), may hold values from -6 to 6
- route_weight: float32 [2048, 8], P('expert'), may hold values from 0.05 to 0.5
- expert_ids: int32 [2048, 8], P('expert'), may hold values from 0 to 255, all different within a row; in each aligned block of 256 rows (0 to 255, 256 to 511, ...) at most 12 rows name the same one
- gate_weight: bfloat16 [8, 7168, 512], P('expert', 'fsdp'), may hold values from -0.0625 to 0.0625
- up_weight: bfloat16 [8, 7168, 512], P('expert', 'fsdp'), may hold values from -0.0625 to 0.0625
- down_weight: bfloat16 [8, 512, 7168], P('expert', None, 'fsdp'), may hold values from -0.1875 to 0.1875
Outputs:
- token_grad: bfloat16 [2048, 7168], P('expert', 'fsdp')
- gate_grad: bfloat16 [8, 7168, 512], P('expert', 'fsdp')
- up_grad: bfloat16 [8, 7168, 512], P('expert', 'fsdp')
- down_grad: bfloat16 [8, 512, 7168], P('expert', None, 'fsdp')
Inputs may be any that keep to these rules, and one draw needn't show every extreme that they name: `expert_ids`: in each block of 256 rows (the tokens held by one position along `expert` (one block of 256 consecutive rows)) no expert is named by more than 12 rows, a bound that some block reaches.
All inputs are finite; a program needn't handle non-finite values.
Results may differ from a plain program's by a relative error of at most 0.025.
Values may be sent and summed in bfloat16 or wider, within the bound.
No kernel may reach another device: no remote copies, remote signals or barrier semaphores. Data moves between devices by JAX's collectives and lax.ppermute only.
A program may use at most 64 MiB of HBM per device.

v0:
```python
import jax
import jax.numpy as jnp
from jax import lax
from jax.sharding import PartitionSpec as P

CAP = 12


def swiglu_grads(gate, up_value, hidden_grad):
    sigmoid_gate = jax.nn.sigmoid(gate)
    activation = (gate * sigmoid_gate * up_value).astype(jnp.bfloat16)
    gate_delta = (
        hidden_grad * up_value * sigmoid_gate * (1.0 + gate * (1.0 - sigmoid_gate))
    ).astype(jnp.bfloat16)
    up_delta = (hidden_grad * gate * sigmoid_gate).astype(jnp.bfloat16)
    return (activation, gate_delta, up_delta)


def body(tokens, output_grad, route_weight, expert_ids, gate_weight, up_weight, down_weight):
    expert_count = lax.axis_size("expert")
    window = expert_count // 2
    tok_rows, top_count = expert_ids.shape
    slab_width = tokens.shape[1]
    slot_count = expert_count * CAP
    send_count = window * CAP
    in_window = expert_ids < window
    expert_hits = (
        expert_ids[:, :, None] == jnp.arange(window, dtype=jnp.int32)[None, None, :]
    ).astype(jnp.int32)
    flat_hits = expert_hits.reshape(tok_rows * top_count, window)
    earlier = jnp.cumsum(flat_hits, axis=0) - flat_hits
    slot_rank = jnp.sum(earlier * flat_hits, axis=1).reshape(tok_rows, top_count)
    slot_ids = jnp.where(in_window, expert_ids * CAP + slot_rank, -1)
    matches = slot_ids[None, :, :] == jnp.arange(send_count, dtype=jnp.int32)[:, None, None]
    placing = jnp.sum(matches.astype(jnp.float32), axis=2).astype(jnp.bfloat16)
    weighted = jnp.sum(jnp.where(matches, route_weight[None, :, :], 0.0), axis=2)
    sent_rows = jnp.dot(placing, tokens, preferred_element_type=jnp.float32).astype(jnp.bfloat16)
    sent_grads = jnp.dot(
        weighted, output_grad.astype(jnp.float32), precision=lax.Precision.HIGHEST
    ).astype(jnp.bfloat16)
    paired_rows = jnp.repeat(sent_rows.reshape(window, CAP, slab_width), 2, axis=0)
    paired_grads = jnp.repeat(sent_grads.reshape(window, CAP, slab_width), 2, axis=0)
    recv_rows, recv_grads = (
        lax.all_to_all(paired_rows, "expert", split_axis=0, concat_axis=0, tiled=True),
        lax.all_to_all(paired_grads, "expert", split_axis=0, concat_axis=0, tiled=True),
    )
    rows = recv_rows.reshape(slot_count, slab_width)
    grads = recv_grads.reshape(slot_count, slab_width)
    gate_w = gate_weight[0]
    up_w = up_weight[0]
    down_w = down_weight[0]
    hidden_width = gate_w.shape[1]
    over_rows = (((0,), (0,)), ((), ()))
    over_columns = (((1,), (1,)), ((), ()))
    gate_part = jnp.dot(rows, gate_w, preferred_element_type=jnp.float32)
    up_part = jnp.dot(rows, up_w, preferred_element_type=jnp.float32)
    hidden_part = lax.dot_general(grads, down_w, over_columns, preferred_element_type=jnp.float32)
    gate_sum, up_sum = (
        lax.psum(gate_part.astype(jnp.bfloat16), "fsdp").astype(jnp.float32),
        lax.psum(up_part.astype(jnp.bfloat16), "fsdp").astype(jnp.float32),
    )
    hidden_share = lax.psum_scatter(
        hidden_part.astype(jnp.bfloat16), "fsdp", scatter_dimension=1, tiled=True
    ).astype(jnp.float32)
    share_width = hidden_width // lax.axis_size("fsdp")
    share_start = lax.axis_index("fsdp") * share_width
    gate_share = lax.dynamic_slice_in_dim(gate_sum, share_start, share_width, 1)
    up_share = lax.dynamic_slice_in_dim(up_sum, share_start, share_width, 1)
    activation = (gate_sum * jax.nn.sigmoid(gate_sum) * up_sum).astype(jnp.bfloat16)
    unused, gate_piece, up_piece = swiglu_grads(gate_share, up_share, hidden_share)
    gate_delta, up_delta = (
        lax.all_gather(gate_piece, "fsdp", axis=1, tiled=True),
        lax.all_gather(up_piece, "fsdp", axis=1, tiled=True),
    )
    down_grad = lax.dot_general(
        activation, grads, over_rows, preferred_element_type=jnp.float32
    ).astype(jnp.bfloat16)
    gate_grad = lax.dot_general(
        rows, gate_delta, over_rows, preferred_element_type=jnp.float32
    ).astype(jnp.bfloat16)
    up_grad = lax.dot_general(rows, up_delta, over_rows, preferred_element_type=jnp.float32).astype(
        jnp.bfloat16
    )
    back_rows = lax.dot_general(
        gate_delta, gate_w, over_columns, preferred_element_type=jnp.float32
    )
    back_rows = (
        back_rows
        + lax.dot_general(up_delta, up_w, over_columns, preferred_element_type=jnp.float32)
    ).astype(jnp.bfloat16)
    returned = lax.all_to_all(
        back_rows.reshape(expert_count, CAP, slab_width),
        "expert",
        split_axis=0,
        concat_axis=0,
        tiled=True,
    )
    halves = returned.reshape(window, 2, CAP, slab_width)
    first_half = halves[:, 0].reshape(send_count, slab_width)
    second_half = halves[:, 1].reshape(send_count, slab_width)
    token_total = lax.dot_general(
        placing, first_half, over_rows, preferred_element_type=jnp.float32
    )
    token_total = token_total + lax.dot_general(
        placing, second_half, over_rows, preferred_element_type=jnp.float32
    )
    token_grad = token_total.astype(jnp.bfloat16)
    return (token_grad, gate_grad[None], up_grad[None], down_grad[None])


def solution(mesh):
    placed = (
        P("expert", "fsdp"),
        P("expert", "fsdp"),
        P("expert", None),
        P("expert", None),
        P("expert", "fsdp", None),
        P("expert", "fsdp", None),
        P("expert", None, "fsdp"),
    )
    return jax.shard_map(
        body,
        mesh=mesh,
        in_specs=placed,
        out_specs=(
            P("expert", "fsdp"),
            P("expert", "fsdp", None),
            P("expert", "fsdp", None),
            P("expert", None, "fsdp"),
        ),
        check_vma=False,
    )
```

profile of v0, /device:TPU:0, one launch (start us, length us, event | category | flops | bytes accessed | tf_op | source)
XLA Modules:
  0.0 140.8 jit_solution(10445876984155720721)
XLA Ops:
  7.2 0.0 copy-start
  7.2 1.0 copy.40
  8.1 0.1 eq.43
  8.3 0.1 eq.39
  8.4 1.2 reduce-window.6
  9.5 0.2 slice_reduce_fusion
  9.7 0.2 reduce-window.9
  9.9 0.1 add_bitcast_fusion
  10.1 0.1 reshape.56
  10.2 0.1 copy.42
  10.2 0.7 add_select_fusion
  10.9 0.9 convert_reduce_fusion
  11.9 1.5 %convolution_convert_fusion.3 = bf16[48,1792]{1,0:T(8,128)(2,1)S(1)} fusion(bf16[256,1792]{1,0:T(8,128)(2,1)} %param.7, bf16[48,256]{1,0:T(8,128)(2,1)S(1)} %get-tuple-element.4), kind=kOutput, calls=%fused_computation.10 | convolution fusion | flops 44126208 | bytes 1114112 | tf_op jit(solution)/shard_map/dot_general | solution.py:37
  13.4 0.8 broadcast_in_dim.40
  14.2 7.3 %all-to-all-start.1 = ((bf16[8,12,1792]{2,1,0:T(8,128)(2,1)}), bf16[8,12,1792]{2,1,0:T(8,128)(2,1)S(1)}, u32[]{:S(2)}, u32[]{:S(2)}) async-start(bf16[8,12,1792]{2,1,0:T(8,128)(2,1)} %bitcast.3), calls=%async_computation.1 | async-start | bytes 917504 | tf_op jit(solution)/shard_map/all_to_all | solution.py:44
  21.5 1.8 %convolution_convert_fusion.4 = bf16[48,1792]{1,0:T(8,128)(2,1)S(1)} fusion(f32[48,256]{1,0:T(8,128)S(1)} %get-tuple-element.5, bf16[256,1792]{1,0:T(8,128)(2,1)} %param.8), kind=kOutput, calls=%fused_computation.11 | convolution fusion | flops 264327168 | bytes 1138688 | tf_op jit(solution)/shard_map/dot_general | solution.py:38
  23.3 11.3 %all-to-all-done.1 = bf16[8,12,1792]{2,1,0:T(8,128)(2,1)S(1)} async-done(((bf16[8,12,1792]{2,1,0:T(8,128)(2,1)}), bf16[8,12,1792]{2,1,0:T(8,128)(2,1)S(1)}, u32[]{:S(2)}, u32[]{:S(2)}) %all-to-all-start.1) | async-done | bytes 344096 | tf_op jit(solution)/shard_map/all_to_all | solution.py:44
  34.6 0.8 broadcast_in_dim.39
  35.4 3.6 %all-to-all-start = ((bf16[8,12,1792]{2,1,0:T(8,128)(2,1)}), bf16[8,12,1792]{2,1,0:T(8,128)(2,1)S(1)}, u32[]{:S(2)}, u32[]{:S(2)}) async-start(bf16[8,12,1792]{2,1,0:T(8,128)(2,1)} %bitcast.1), calls=%async_computation | async-start | bytes 917504 | tf_op jit(solution)/shard_map/all_to_all | solution.py:45
  39.0 0.0 all-reduce.3.cloned.1.call-start
  39.0 0.1 reshape.62
  39.2 1.1 fusion.20
  40.2 0.5 copy-done.1
  40.7 1.1 fusion.17
  41.8 0.0 all-reduce.3.cloned.1.call-update
  41.8 0.0 reduce-scatter.4.cloned.1.call-start
  41.8 10.3 %all-to-all-done = bf16[8,12,1792]{2,1,0:T(8,128)(2,1)S(1)} async-done(((bf16[8,12,1792]{2,1,0:T(8,128)(2,1)}), bf16[8,12,1792]{2,1,0:T(8,128)(2,1)S(1)}, u32[]{:S(2)}, u32[]{:S(2)}) %all-to-all-start) | async-done | bytes 344096 | tf_op jit(solution)/shard_map/all_to_all | solution.py:45
  52.2 0.1 reshape.59
  52.3 2.2 %fusion.14 = bf16[96,512]{1,0:T(8,128)(2,1)S(1)} fusion(bf16[96,1792]{1,0:T(8,128)(2,1)S(1)} %reshape.59, bf16[1,512,1792]{2,1,0:T(8,128)(2,1)} %param.13), kind=kOutput, calls=%fused_computation.21 | convolution fusion | flops 176209920 | bytes 2277376 | tf_op jit(solution)/shard_map/dot_general | solution.py:57
  54.5 0.8 copy.45
  55.2 0.0 reduce-scatter.4.cloned.1.call-update
  55.3 21.0 %all-reduce.3.cloned.1.call-done = (bf16[96,512]{1,0:T(8,128)(2,1)}, bf16[96,512]{1,0:T(8,128)(2,1)}) async-done(((bf16[96,512]{1,0:T(8,128)(2,1)}, bf16[96,512]{1,0:T(8,128)(2,1)}), (bf16[96,512]{1,0:T(8,128)(2,1)}, bf16[96,512]{1,0:T(8,128)(2,1)})) %all-reduce.3.cloned.1.call-update) | async-done | bytes 196624 | tf_op jit(solution)/shard_map/psum | solution.py:60
  76.3 0.9 convert_element_type.72
  77.2 0.9 convert_element_type.74
  78.1 20.8 %reduce-scatter.4.cloned.1.call-done = bf16[128,96]{1,0:T(8,128)(2,1)} async-done(((bf16[512,96]{1,0:T(8,128)(2,1)}), bf16[128,96]{1,0:T(8,128)(2,1)}) %reduce-scatter.4.cloned.1.call-update) | async-done | bytes 24592
  98.9 0.8 copy.46
  99.9 5.5 %all_gather.7 = bf16[96,512]{1,0:T(8,128)(2,1)S(1)} all-gather(bf16[96,128]{1,0:T(8,128)(2,1)S(1)} %get-tuple-element.10), channel_id=1, replica_groups=mesh['expert'=8,'fsdp'=4] {'fsdp'}, dimensions={1}, use_global_device_ids=true | all-gather | bytes 122880 | tf_op jit(solution)/shard_map/all_gather | solution.py:73
  105.3 5.3 %all_gather.6 = bf16[96,512]{1,0:T(8,128)(2,1)S(1)} all-gather(bf16[96,128]{1,0:T(8,128)(2,1)S(1)} %get-tuple-element.11), channel_id=1, replica_groups=mesh['expert'=8,'fsdp'=4] {'fsdp'}, dimensions={1}, use_global_device_ids=true | all-gather | bytes 122880 | tf_op jit(solution)/shard_map/all_gather | solution.py:72
  110.7 0.7 fusion.5
  111.4 0.7 fusion.4
  112.1 0.9 reshape.63
  112.9 5.5 %all-to-all-start.2 = ((bf16[8,12,1792]{2,1,0:T(8,128)(2,1)}), bf16[8,12,1792]{2,1,0:T(8,128)(2,1)S(1)}, u32[]{:S(2)}, u32[]{:S(2)}) async-start(bf16[8,12,1792]{2,1,0:T(8,128)(2,1)} %reshape.63), calls=%async_computation.2 | async-start | bytes 917504 | tf_op jit(solution)/shard_map/all_to_all | solution.py:91
  118.5 1.9 %fusion.2 = bf16[1,512,1792]{2,1,0:T(8,128)(2,1)} fusion(bf16[96,1792]{1,0:T(8,128)(2,1)S(1)} %reshape.59, bf16[96,512]{1,0:T(8,128)(2,1)S(1)} %copy-done.4, bf16[96,512]{1,0:T(8,128)(2,1)S(1)} %copy-done.3), kind=kOutput, calls=%fused_computation.6 | convolution fusion | flops 177471488 | bytes 2375680 | tf_op jit(solution)/shard_map/dot_general | solution.py:75
  120.4 1.9 %fusion.1 = bf16[1,1792,512]{2,1,0:T(8,128)(2,1)} fusion(bf16[96,1792]{1,0:T(8,128)(2,1)S(1)} %reshape.62, bf16[96,512]{1,0:T(8,128)(2,1)S(1)} %all_gather.7), kind=kOutput, calls=%fused_computation.5 | convolution fusion | flops 177078272 | bytes 2277376 | tf_op jit(solution)/shard_map/dot_general | solution.py:81
  122.3 1.9 %fusion = bf16[1,1792,512]{2,1,0:T(8,128)(2,1)} fusion(bf16[96,1792]{1,0:T(8,128)(2,1)S(1)} %reshape.62, bf16[96,512]{1,0:T(8,128)(2,1)S(1)} %all_gather.6), kind=kOutput, calls=%fused_computation.4 | convolution fusion | flops 177078272 | bytes 2277376 | tf_op jit(solution)/shard_map/dot_general | solution.py:78
  124.2 7.9 %all-to-all-done.2 = bf16[8,12,1792]{2,1,0:T(8,128)(2,1)S(1)} async-done(((bf16[8,12,1792]{2,1,0:T(8,128)(2,1)}), bf16[8,12,1792]{2,1,0:T(8,128)(2,1)S(1)}, u32[]{:S(2)}, u32[]{:S(2)}) %all-to-all-start.2) | async-done | bytes 344096 | tf_op jit(solution)/shard_map/all_to_all | solution.py:91
  132.2 0.4 fusion.40
  132.6 1.3 fusion.3
  (16 shorter events, 0.3 us)
Async XLA Ops:
  7.2 32.0 %copy-start = (bf16[1,1792,512]{2,1,0:T(8,128)(2,1)S(1)}, bf16[1,1792,512]{2,1,0:T(8,128)(2,1)}, u32[]{:S(2)}) copy-start(bf16[1,1792,512]{2,1,0:T(8,128)(2,1)} %param.11) | copy-start | bytes 5505028
  14.2 20.4 %all-to-all-start.1 = ((bf16[8,12,1792]{2,1,0:T(8,128)(2,1)}), bf16[8,12,1792]{2,1,0:T(8,128)(2,1)S(1)}, u32[]{:S(2)}, u32[]{:S(2)}) async-start(bf16[8,12,1792]{2,1,0:T(8,128)(2,1)} %bitcast.3), calls=%async_computation.1 | async-start | bytes 917504 | tf_op jit(solution)/shard_map/all_to_all | solution.py:44
  35.4 16.8 %all-to-all-start = ((bf16[8,12,1792]{2,1,0:T(8,128)(2,1)}), bf16[8,12,1792]{2,1,0:T(8,128)(2,1)S(1)}, u32[]{:S(2)}, u32[]{:S(2)}) async-start(bf16[8,12,1792]{2,1,0:T(8,128)(2,1)} %bitcast.1), calls=%async_computation | async-start | bytes 917504 | tf_op jit(solution)/shard_map/all_to_all | solution.py:45
  39.0 37.3 %all-reduce.3.cloned.1.call-start = ((), (), s32[]{:S(2)}) async-start(), calls=%async_computation.5 | async-start | bytes 393216 | tf_op jit(solution)/shard_map/psum | solution.py:60
  39.1 1.5 %copy-start.1 = (bf16[1,1792,512]{2,1,0:T(8,128)(2,1)S(1)}, bf16[1,1792,512]{2,1,0:T(8,128)(2,1)}, u32[]{:S(2)}) copy-start(bf16[1,1792,512]{2,1,0:T(8,128)(2,1)} %param.12) | copy-start | bytes 5505028
  41.8 57.1 %reduce-scatter.4.cloned.1.call-start = ((), (), s32[]{:S(2)}) async-start(), calls=%async_computation.4 | async-start | bytes 163840
  99.8 11.6 %copy-start.2 = (bf16[1,1792,512]{2,1,0:T(8,128)(2,1)S(1)}, bf16[1,1792,512]{2,1,0:T(8,128)(2,1)}, u32[]{:S(2)}) copy-start(bf16[1,1792,512]{2,1,0:T(8,128)(2,1)} %param.12) | copy-start | bytes 5505028
  111.4 7.1 %copy-start.3 = (bf16[96,512]{1,0:T(8,128)(2,1)S(1)}, bf16[96,512]{1,0:T(8,128)(2,1)}, u32[]{:S(2)}) copy-start(bf16[96,512]{1,0:T(8,128)(2,1)} %get-tuple-element.6) | copy-start | bytes 294916
  111.4 7.1 %copy-start.4 = (bf16[96,512]{1,0:T(8,128)(2,1)S(1)}, bf16[96,512]{1,0:T(8,128)(2,1)}, u32[]{:S(2)}) copy-start(bf16[96,512]{1,0:T(8,128)(2,1)} %get-tuple-element.7) | copy-start | bytes 294916
  112.9 19.1 %all-to-all-start.2 = ((bf16[8,12,1792]{2,1,0:T(8,128)(2,1)}), bf16[8,12,1792]{2,1,0:T(8,128)(2,1)S(1)}, u32[]{:S(2)}, u32[]{:S(2)}) async-start(bf16[8,12,1792]{2,1,0:T(8,128)(2,1)} %reshape.63), calls=%async_computation.2 | async-start | bytes 917504 | tf_op jit(solution)/shard_map/all_to_all | solution.py:91
Sparse Core Ops, SparseCore 0:
  42.7 33.5 all-reduce.2
  79.3 19.6 reduce-scatter.3
where the time goes:
time: 142 us; the launch traced here: 141 us
  waiting for transfers between devices  71.4 us (50%)
  starting transfers between devices  16.5 us (12%)
  matrix products  16.4 us (12%)
  between operations  14.2 us (10%)
  blocking collectives  10.8 us (8%)
  local copies, waits for them, and re-layouts  6.46 us (5%)
  other arithmetic  4.98 us (4%)
    psum x1, waiting for transfers between devices, body(): lax.psum(up_part.astype(jnp.bfloat16), 'fsdp').astype(jnp.float32)  21 us
    unnamed x3, waiting for transfers between devices  20.9 us
    all_to_all x1, waiting for transfers between devices, body(): lax.all_to_all(paired_rows, 'expert', split_axis=0, concat_axis=0, tiled=...  11.3 us
    all_to_all x1, waiting for transfers between devices, body(): lax.all_to_all(paired_grads, 'expert', split_axis=0, concat_axis=0, tiled...  10.3 us
    all_to_all x1, waiting for transfers between devices, body(): lax.all_to_all(back_rows.reshape(expert_count, CAP, slab_width), 'expert'...  7.87 us
    all_to_all x1, starting transfers between devices, body(): lax.all_to_all(paired_rows, 'expert', split_axis=0, concat_axis=0, tiled=...  7.28 us
    all_to_all x1, starting transfers between devices, body(): lax.all_to_all(back_rows.reshape(expert_count, CAP, slab_width), 'expert'...  5.51 us
    all_gather x1, blocking collectives, body(): lax.all_gather(up_piece, 'fsdp', axis=1, tiled=True)  5.49 us
  transfers between devices with their start and end apart: 5, of which 5 were waited for; matrix products, arithmetic and copies ran while one was open for 10% of the time, Pallas kernels for 0%

commit v1 on v0

--- a/solution.py
+++ b/solution.py
@@ -4,6 +4,22 @@
 from jax.sharding import PartitionSpec as P
 
 CAP = 12
+
+
+def exchange_in_pairs(array, axis, split, join):
+    ways, here = (lax.axis_size(axis), lax.axis_index(axis))
+    width = array.shape[split] // ways
+    dims = list(array.shape)
+    dims[split] = width
+    height = dims[join]
+    dims[join] = height * ways
+    full = jnp.zeros(dims, array.dtype)
+    for mask in range(ways):
+        part = lax.dynamic_slice_in_dim(array, (here ^ mask) * width, width, axis=split)
+        if mask:
+            part = lax.ppermute(part, axis, [(d, d ^ mask) for d in range(ways)])
+        full = lax.dynamic_update_slice_in_dim(full, part, (here ^ mask) * height, axis=join)
+    return full
 
 
 def swiglu_grads(gate, up_value, hidden_grad):
@@ -41,7 +57,7 @@
     paired_rows = jnp.repeat(sent_rows.reshape(window, CAP, slab_width), 2, axis=0)
     paired_grads = jnp.repeat(sent_grads.reshape(window, CAP, slab_width), 2, axis=0)
     recv_rows, recv_grads = (
-        lax.all_to_all(paired_rows, "expert", split_axis=0, concat_axis=0, tiled=True),
+        exchange_in_pairs(paired_rows, "expert", 0, 0),
         lax.all_to_all(paired_grads, "expert", split_axis=0, concat_axis=0, tiled=True),
     )
     rows = recv_rows.reshape(slot_count, slab_width)

time: 142 us -> 147 us (1.035)
  starting transfers between devices: 16.5 us -> 26.1 us
  waiting for transfers between devices: 71.4 us -> 66.1 us
    ppermute x0 -> x7, starting transfers between devices: none -> 15.6 us  [exchange_in_pairs(): part = lax.ppermute(part, axis, [(d, d ^ mask) for d in range(ways)])]
    all_to_all x1 -> x0, waiting for transfers between devices: 11.3 us -> none  [body(): lax.all_to_all(paired_rows, 'expert', split_axis=0, concat_axis=0, tiled=...]
    all_to_all x1, waiting for transfers between devices: 10.3 us -> 0.01 us  [body(): lax.all_to_all(paired_grads, 'expert', split_axis=0, concat_axis=0, tiled...]
    ppermute x0 -> x7, waiting for transfers between devices: none -> 9.38 us  [exchange_in_pairs(): part = lax.ppermute(part, axis, [(d, d ^ mask) for d in range(ways)])]
    all_to_all x1 -> x0, starting transfers between devices: 7.28 us -> none  [body(): lax.all_to_all(paired_rows, 'expert', split_axis=0, concat_axis=0, tiled=...]
    psum x1, waiting for transfers between devices: 21 us -> 28 us  [body(): lax.psum(up_part.astype(jnp.bfloat16), 'fsdp').astype(jnp.float32)]
  transfers between devices with their start and end apart: 5 -> 11, of which waited for: 5 -> 7; matrix products, arithmetic and copies ran while one was open for 10% -> 11% of each run, Pallas kernels for 0% -> 0%
where the time goes in v1:
time: 147 us; the launch traced here: 146 us
  waiting for transfers between devices  66.1 us (45%)
  starting transfers between devices  26.1 us (18%)
  matrix products  16.4 us (11%)
  between operations  14.4 us (10%)
  blocking collectives  10.8 us (7%)
  local copies, waits for them, and re-layouts  7.26 us (5%)
  other arithmetic  4.98 us (3%)
    psum x1, waiting for transfers between devices, body(): lax.psum(up_part.astype(jnp.bfloat16), 'fsdp').astype(jnp.float32)  28 us
    unnamed x3, waiting for transfers between devices  20.9 us
    ppermute x7, starting transfers between devices, exchange_in_pairs(): part = lax.ppermute(part, axis, [(d, d ^ mask) for d in range(ways)])  15.6 us
    ppermute x7, waiting for transfers between devices, exchange_in_pairs(): part = lax.ppermute(part, axis, [(d, d ^ mask) for d in range(ways)])  9.38 us
    all_to_all x1, waiting for transfers between devices, body(): lax.all_to_all(back_rows.reshape(expert_count, CAP, slab_width), 'expert'...  7.87 us
    all_to_all x1, starting transfers between devices, body(): lax.all_to_all(back_rows.reshape(expert_count, CAP, slab_width), 'expert'...  5.51 us
    all_gather x1, blocking collectives, body(): lax.all_gather(up_piece, 'fsdp', axis=1, tiled=True)  5.49 us
    all_gather x1, blocking collectives, body(): lax.all_gather(gate_piece, 'fsdp', axis=1, tiled=True)  5.34 us
  transfers between devices with their start and end apart: 11, of which 7 were waited for; matrix products, arithmetic and copies ran while one was open for 11% of the time, Pallas kernels for 0%

profile of v1, /device:TPU:0, one launch (start us, length us, event | category | flops | bytes accessed | tf_op | source)
XLA Modules:
  0.0 146.0 jit_solution(5459413489291548880)
XLA Ops:
  7.2 0.9 copy.40
  8.2 0.1 eq.43
  8.3 0.1 eq.39
  8.4 1.2 reduce-window.6
  9.6 0.2 slice_reduce_fusion
  9.8 0.2 reduce-window.9
  10.1 0.1 reshape.56
  10.3 0.7 add_select_fusion
  11.0 0.9 convert_reduce_fusion
  11.9 1.5 %convolution_convert_fusion.3 = bf16[48,1792]{1,0:T(8,128)(2,1)S(1)} fusion(bf16[256,1792]{1,0:T(8,128)(2,1)} %param.7, bf16[48,256]{1,0:T(8,128)(2,1)S(1)} %get-tuple-element.4), kind=kOutput, calls=%fused_computation.10 | convolution fusion | flops 44126208 | bytes 1114112 | tf_op jit(solution)/shard_map/dot_general | solution.py:53
  13.5 0.7 constant_dynamic-slice_fusion
  14.2 3.0 %collective-permute-start = (bf16[1,12,1792]{2,1,0:T(8,128)(2,1)}, bf16[1,12,1792]{2,1,0:T(8,128)(2,1)}, u32[]{:S(2)}, u32[]{:S(2)}) collective-permute-start(bf16[1,12,1792]{2,1,0:T(8,128)(2,1)} %get-tuple-element.16), channel_id=1, source_target_pairs={{0,4},{4,0},{8,12},{12,8},{16,20},{20,16},{24,28},{28,24},{1,5},{5... | collective-permute-start | bytes 129032 | tf_op jit(solution)/shard_map/ppermute | solution.py:20
  17.2 1.8 %convolution_convert_fusion.4 = bf16[48,1792]{1,0:T(8,128)(2,1)S(1)} fusion(f32[48,256]{1,0:T(8,128)S(1)} %get-tuple-element.5, bf16[256,1792]{1,0:T(8,128)(2,1)} %param.8), kind=kOutput, calls=%fused_computation.11 | convolution fusion | flops 264327168 | bytes 1138688 | tf_op jit(solution)/shard_map/dot_general | solution.py:54
  19.0 0.8 broadcast_in_dim.42
  19.8 4.9 %all-to-all-start = ((bf16[8,12,1792]{2,1,0:T(8,128)(2,1)}), bf16[8,12,1792]{2,1,0:T(8,128)(2,1)S(1)}, u32[]{:S(2)}, u32[]{:S(2)}) async-start(bf16[8,12,1792]{2,1,0:T(8,128)(2,1)} %bitcast.1), calls=%async_computation | async-start | bytes 917504 | tf_op jit(solution)/shard_map/all_to_all | solution.py:61
  24.7 4.7 %collective-permute-start.6 = (bf16[1,12,1792]{2,1,0:T(8,128)(2,1)S(1)}, bf16[1,12,1792]{2,1,0:T(8,128)(2,1)S(1)}, u32[]{:S(2)}, u32[]{:S(2)}) collective-permute-start(bf16[1,12,1792]{2,1,0:T(8,128)(2,1)S(1)} %get-tuple-element.10), channel_id=1, source_target_pairs={{0,28},{4,24},{8,20},{12,16},{16,12},{20,8},{24,4},{28,0},{1,29},{... | collective-permute-start | bytes 129032 | tf_op jit(solution)/shard_map/ppermute | solution.py:20
  29.4 0.6 collective-permute-start.5
  30.0 0.6 collective-permute-start.4
  30.5 1.9 %collective-permute-start.3 = (bf16[1,12,1792]{2,1,0:T(8,128)(2,1)S(1)}, bf16[1,12,1792]{2,1,0:T(8,128)(2,1)S(1)}, u32[]{:S(2)}, u32[]{:S(2)}) collective-permute-start(bf16[1,12,1792]{2,1,0:T(8,128)(2,1)S(1)} %get-tuple-element.13), channel_id=1, source_target_pairs={{0,16},{4,20},{8,24},{12,28},{16,0},{20,4},{24,8},{28,12},{1,17},{... | collective-permute-start | bytes 129032 | tf_op jit(solution)/shard_map/ppermute | solution.py:20
  32.4 1.4 collective-permute-start.1
  33.8 0.8 constant_dynamic-update-slice_fusion.6
  34.6 3.5 %collective-permute-done.1 = bf16[1,12,1792]{2,1,0:T(8,128)(2,1)S(1)} collective-permute-done((bf16[1,12,1792]{2,1,0:T(8,128)(2,1)S(1)}, bf16[1,12,1792]{2,1,0:T(8,128)(2,1)S(1)}, u32[]{:S(2)}, u32[]{:S(2)}) %collective-permute-start.1) | collective-permute-done | bytes 43040 | tf_op jit(solution)/shard_map/ppermute | solution.py:20
  38.2 3.6 %collective-permute-start.2 = (bf16[1,12,1792]{2,1,0:T(8,128)(2,1)S(1)}, bf16[1,12,1792]{2,1,0:T(8,128)(2,1)S(1)}, u32[]{:S(2)}, u32[]{:S(2)}) collective-permute-start(bf16[1,12,1792]{2,1,0:T(8,128)(2,1)S(1)} %get-tuple-element.14), channel_id=1, source_target_pairs={{0,12},{4,8},{8,4},{12,0},{16,28},{20,24},{24,20},{28,16},{1,13},{... | collective-permute-start | bytes 129032 | tf_op jit(solution)/shard_map/ppermute | solution.py:20
  41.7 2.7 %collective-permute-done.2 = bf16[1,12,1792]{2,1,0:T(8,128)(2,1)S(1)} collective-permute-done((bf16[1,12,1792]{2,1,0:T(8,128)(2,1)S(1)}, bf16[1,12,1792]{2,1,0:T(8,128)(2,1)S(1)}, u32[]{:S(2)}, u32[]{:S(2)}) %collective-permute-start.2) | collective-permute-done | bytes 43040 | tf_op jit(solution)/shard_map/ppermute | solution.py:20
  44.4 2.9 %collective-permute-done.3 = bf16[1,12,1792]{2,1,0:T(8,128)(2,1)S(1)} collective-permute-done((bf16[1,12,1792]{2,1,0:T(8,128)(2,1)S(1)}, bf16[1,12,1792]{2,1,0:T(8,128)(2,1)S(1)}, u32[]{:S(2)}, u32[]{:S(2)}) %collective-permute-start.3) | collective-permute-done | bytes 43040 | tf_op jit(solution)/shard_map/ppermute | solution.py:20
  47.4 0.2 collective-permute-done.4
  47.8 1.1 fusion.20
  48.8 0.5 copy-done.1
  49.3 1.1 fusion.17
  50.5 2.2 %fusion.14 = bf16[96,512]{1,0:T(8,128)(2,1)S(1)} fusion(bf16[96,1792]{1,0:T(8,128)(2,1)S(1)} %reshape.59, bf16[1,512,1792]{2,1,0:T(8,128)(2,1)} %param.13), kind=kOutput, calls=%fused_computation.21 | convolution fusion | flops 176209920 | bytes 2277376 | tf_op jit(solution)/shard_map/dot_general | solution.py:73
  52.7 0.8 copy.45
  53.5 28.0 %all-reduce.3.cloned.1.call-done = (bf16[96,512]{1,0:T(8,128)(2,1)}, bf16[96,512]{1,0:T(8,128)(2,1)}) async-done(((bf16[96,512]{1,0:T(8,128)(2,1)}, bf16[96,512]{1,0:T(8,128)(2,1)}), (bf16[96,512]{1,0:T(8,128)(2,1)}, bf16[96,512]{1,0:T(8,128)(2,1)})) %all-reduce.3.cloned.1.call-update) | async-done | bytes 196624 | tf_op jit(solution)/shard_map/psum | solution.py:76
  81.5 0.9 convert_element_type.72
  82.4 0.9 convert_element_type.74
  83.3 20.8 %reduce-scatter.4.cloned.1.call-done = bf16[128,96]{1,0:T(8,128)(2,1)} async-done(((bf16[512,96]{1,0:T(8,128)(2,1)}), bf16[128,96]{1,0:T(8,128)(2,1)}) %reduce-scatter.4.cloned.1.call-update) | async-done | bytes 24592
  104.2 0.8 copy.46
  105.1 5.5 %all_gather.7 = bf16[96,512]{1,0:T(8,128)(2,1)S(1)} all-gather(bf16[96,128]{1,0:T(8,128)(2,1)S(1)} %get-tuple-element.18), channel_id=1, replica_groups=mesh['expert'=8,'fsdp'=4] {'fsdp'}, dimensions={1}, use_global_device_ids=true | all-gather | bytes 122880 | tf_op jit(solution)/shard_map/all_gather | solution.py:89
  110.6 5.3 %all_gather.6 = bf16[96,512]{1,0:T(8,128)(2,1)S(1)} all-gather(bf16[96,128]{1,0:T(8,128)(2,1)S(1)} %get-tuple-element.19), channel_id=1, replica_groups=mesh['expert'=8,'fsdp'=4] {'fsdp'}, dimensions={1}, use_global_device_ids=true | all-gather | bytes 122880 | tf_op jit(solution)/shard_map/all_gather | solution.py:88
  115.9 0.7 fusion.5
  116.6 0.7 fusion.4
  117.3 0.9 reshape.63
  118.2 5.5 %all-to-all-start.1 = ((bf16[8,12,1792]{2,1,0:T(8,128)(2,1)}), bf16[8,12,1792]{2,1,0:T(8,128)(2,1)S(1)}, u32[]{:S(2)}, u32[]{:S(2)}) async-start(bf16[8,12,1792]{2,1,0:T(8,128)(2,1)} %reshape.63), calls=%async_computation.1 | async-start | bytes 917504 | tf_op jit(solution)/shard_map/all_to_all | solution.py:107
  123.7 1.9 %fusion.2 = bf16[1,512,1792]{2,1,0:T(8,128)(2,1)} fusion(bf16[96,1792]{1,0:T(8,128)(2,1)S(1)} %reshape.59, bf16[96,512]{1,0:T(8,128)(2,1)S(1)} %copy-done.4, bf16[96,512]{1,0:T(8,128)(2,1)S(1)} %copy-done.3), kind=kOutput, calls=%fused_computation.6 | convolution fusion | flops 177471488 | bytes 2375680 | tf_op jit(solution)/shard_map/dot_general | solution.py:91
  125.6 1.9 %fusion.1 = bf16[1,1792,512]{2,1,0:T(8,128)(2,1)} fusion(bf16[96,1792]{1,0:T(8,128)(2,1)S(1)} %reshape.62, bf16[96,512]{1,0:T(8,128)(2,1)S(1)} %all_gather.7), kind=kOutput, calls=%fused_computation.5 | convolution fusion | flops 177078272 | bytes 2277376 | tf_op jit(solution)/shard_map/dot_general | solution.py:97
  127.5 1.9 %fusion = bf16[1,1792,512]{2,1,0:T(8,128)(2,1)} fusion(bf16[96,1792]{1,0:T(8,128)(2,1)S(1)} %reshape.62, bf16[96,512]{1,0:T(8,128)(2,1)S(1)} %all_gather.6), kind=kOutput, calls=%fused_computation.4 | convolution fusion | flops 177078272 | bytes 2277376 | tf_op jit(solution)/shard_map/dot_general | solution.py:94
  129.4 7.9 %all-to-all-done.1 = bf16[8,12,1792]{2,1,0:T(8,128)(2,1)S(1)} async-done(((bf16[8,12,1792]{2,1,0:T(8,128)(2,1)}), bf16[8,12,1792]{2,1,0:T(8,128)(2,1)S(1)}, u32[]{:S(2)}, u32[]{:S(2)}) %all-to-all-start.1) | async-done | bytes 344096 | tf_op jit(solution)/shard_map/all_to_all | solution.py:107
  137.4 0.4 fusion.40
  137.8 1.3 fusion.3
  (37 shorter events, 0.9 us)
Async XLA Ops:
  7.2 40.6 %copy-start = (bf16[1,1792,512]{2,1,0:T(8,128)(2,1)S(1)}, bf16[1,1792,512]{2,1,0:T(8,128)(2,1)}, u32[]{:S(2)}) copy-start(bf16[1,1792,512]{2,1,0:T(8,128)(2,1)} %param.11) | copy-start | bytes 5505028
  14.2 18.2 %collective-permute-start = (bf16[1,12,1792]{2,1,0:T(8,128)(2,1)}, bf16[1,12,1792]{2,1,0:T(8,128)(2,1)}, u32[]{:S(2)}, u32[]{:S(2)}) collective-permute-start(bf16[1,12,1792]{2,1,0:T(8,128)(2,1)} %get-tuple-element.16), channel_id=1, source_target_pairs={{0,4},{4,0},{8,12},{12,8},{16,20},{20,16},{24,28},{28,24},{1,5},{5... | collective-permute-start | bytes 129032 | tf_op jit(solution)/shard_map/ppermute | solution.py:20
  19.8 30.6 %all-to-all-start = ((bf16[8,12,1792]{2,1,0:T(8,128)(2,1)}), bf16[8,12,1792]{2,1,0:T(8,128)(2,1)S(1)}, u32[]{:S(2)}, u32[]{:S(2)}) async-start(bf16[8,12,1792]{2,1,0:T(8,128)(2,1)} %bitcast.1), calls=%async_computation | async-start | bytes 917504 | tf_op jit(solution)/shard_map/all_to_all | solution.py:61
  24.7 56.8 %all-reduce.3.cloned.1.call-start = ((), (), s32[]{:S(2)}) async-start(), calls=%async_computation.4 | async-start | bytes 393216 | tf_op jit(solution)/shard_map/psum | solution.py:76
  24.7 22.9 %collective-permute-start.6 = (bf16[1,12,1792]{2,1,0:T(8,128)(2,1)S(1)}, bf16[1,12,1792]{2,1,0:T(8,128)(2,1)S(1)}, u32[]{:S(2)}, u32[]{:S(2)}) collective-permute-start(bf16[1,12,1792]{2,1,0:T(8,128)(2,1)S(1)} %get-tuple-element.10), channel_id=1, source_target_pairs={{0,28},{4,24},{8,20},{12,16},{16,12},{20,8},{24,4},{28,0},{1,29},{... | collective-permute-start | bytes 129032 | tf_op jit(solution)/shard_map/ppermute | solution.py:20
  29.4 18.2 %collective-permute-start.5 = (bf16[1,12,1792]{2,1,0:T(8,128)(2,1)S(1)}, bf16[1,12,1792]{2,1,0:T(8,128)(2,1)S(1)}, u32[]{:S(2)}, u32[]{:S(2)}) collective-permute-start(bf16[1,12,1792]{2,1,0:T(8,128)(2,1)S(1)} %get-tuple-element.11), channel_id=1, source_target_pairs={{0,24},{4,28},{8,16},{12,20},{16,8},{20,12},{24,0},{28,4},{1,25},{... | collective-permute-start | bytes 129032 | tf_op jit(solution)/shard_map/ppermute | solution.py:20
  30.0 17.6 %collective-permute-start.4 = (bf16[1,12,1792]{2,1,0:T(8,128)(2,1)S(1)}, bf16[1,12,1792]{2,1,0:T(8,128)(2,1)S(1)}, u32[]{:S(2)}, u32[]{:S(2)}) collective-permute-start(bf16[1,12,1792]{2,1,0:T(8,128)(2,1)S(1)} %get-tuple-element.12), channel_id=1, source_target_pairs={{0,20},{4,16},{8,28},{12,24},{16,4},{20,0},{24,12},{28,8},{1,21},{... | collective-permute-start | bytes 129032 | tf_op jit(solution)/shard_map/ppermute | solution.py:20
  30.5 16.8 %collective-permute-start.3 = (bf16[1,12,1792]{2,1,0:T(8,128)(2,1)S(1)}, bf16[1,12,1792]{2,1,0:T(8,128)(2,1)S(1)}, u32[]{:S(2)}, u32[]{:S(2)}) collective-permute-start(bf16[1,12,1792]{2,1,0:T(8,128)(2,1)S(1)} %get-tuple-element.13), channel_id=1, source_target_pairs={{0,16},{4,20},{8,24},{12,28},{16,0},{20,4},{24,8},{28,12},{1,17},{... | collective-permute-start | bytes 129032 | tf_op jit(solution)/shard_map/ppermute | solution.py:20
  32.4 5.7 %collective-permute-start.1 = (bf16[1,12,1792]{2,1,0:T(8,128)(2,1)S(1)}, bf16[1,12,1792]{2,1,0:T(8,128)(2,1)S(1)}, u32[]{:S(2)}, u32[]{:S(2)}) collective-permute-start(bf16[1,12,1792]{2,1,0:T(8,128)(2,1)S(1)} %get-tuple-element.15), channel_id=1, source_target_pairs={{0,8},{4,12},{8,0},{12,4},{16,24},{20,28},{24,16},{28,20},{1,9},{5... | collective-permute-start | bytes 129032 | tf_op jit(solution)/shard_map/ppermute | solution.py:20
  38.2 6.3 %collective-permute-start.2 = (bf16[1,12,1792]{2,1,0:T(8,128)(2,1)S(1)}, bf16[1,12,1792]{2,1,0:T(8,128)(2,1)S(1)}, u32[]{:S(2)}, u32[]{:S(2)}) collective-permute-start(bf16[1,12,1792]{2,1,0:T(8,128)(2,1)S(1)} %get-tuple-element.14), channel_id=1, source_target_pairs={{0,12},{4,8},{8,4},{12,0},{16,28},{20,24},{24,20},{28,16},{1,13},{... | collective-permute-start | bytes 129032 | tf_op jit(solution)/shard_map/ppermute | solution.py:20
  47.8 1.5 %copy-start.1 = (bf16[1,1792,512]{2,1,0:T(8,128)(2,1)S(1)}, bf16[1,1792,512]{2,1,0:T(8,128)(2,1)}, u32[]{:S(2)}) copy-start(bf16[1,1792,512]{2,1,0:T(8,128)(2,1)} %param.12) | copy-start | bytes 5505028
  50.4 53.8 %reduce-scatter.4.cloned.1.call-start = ((), (), s32[]{:S(2)}) async-start(), calls=%async_computation.3 | async-start | bytes 163840
  105.0 11.6 %copy-start.2 = (bf16[1,1792,512]{2,1,0:T(8,128)(2,1)S(1)}, bf16[1,1792,512]{2,1,0:T(8,128)(2,1)}, u32[]{:S(2)}) copy-start(bf16[1,1792,512]{2,1,0:T(8,128)(2,1)} %param.12) | copy-start | bytes 5505028
  116.6 7.1 %copy-start.3 = (bf16[96,512]{1,0:T(8,128)(2,1)S(1)}, bf16[96,512]{1,0:T(8,128)(2,1)}, u32[]{:S(2)}) copy-start(bf16[96,512]{1,0:T(8,128)(2,1)} %get-tuple-element.6) | copy-start | bytes 294916
  116.6 7.1 %copy-start.4 = (bf16[96,512]{1,0:T(8,128)(2,1)S(1)}, bf16[96,512]{1,0:T(8,128)(2,1)}, u32[]{:S(2)}) copy-start(bf16[96,512]{1,0:T(8,128)(2,1)} %get-tuple-element.7) | copy-start | bytes 294916
  118.2 19.1 %all-to-all-start.1 = ((bf16[8,12,1792]{2,1,0:T(8,128)(2,1)}), bf16[8,12,1792]{2,1,0:T(8,128)(2,1)S(1)}, u32[]{:S(2)}, u32[]{:S(2)}) async-start(bf16[8,12,1792]{2,1,0:T(8,128)(2,1)} %reshape.63), calls=%async_computation.1 | async-start | bytes 917504 | tf_op jit(solution)/shard_map/all_to_all | solution.py:107
Sparse Core Ops, SparseCore 0:
  50.5 30.9 all-reduce.2
  84.5 19.6 reduce-scatter.3
